TPU v7x, 32 devices: a whole 2x2x4 slice. The times are simulated.
32 devices in a mesh: groups: 2 (over y), blk: 16 (over z, x, core).
Axes of the slice: x: 2, y: 2, z: 4, core: 2. Of those that a mesh axis runs over, the one named last changes fastest.
Arguments:
- query_hidden: bfloat16 [512, 32, 768], P(('groups', 'blk')), parts along dimension 0, may hold values from -6 to 6
- passage_hidden: bfloat16 [256, 180, 768], P(('groups', 'blk')), parts along dimension 0, may hold values from -6 to 6
- projection: bfloat16 [768, 128], replicated, may hold values from -0.21875 to 0.21875
- teacher_rows: float32 [512, 32], P(('groups', 'blk')), parts along dimension 0, may hold values from -12 to 12
- teacher_pos: int32 [512], P(('groups', 'blk')), parts along dimension 0, may hold values from 0 to 255, each once
- neg_count: int32 [512], P(('groups', 'blk')), parts along dimension 0, may hold values from 8 to 32
- pass_len: int32 [256], P(('groups', 'blk')), parts along dimension 0, may hold values from 19 to 180
Outputs:
- loss: float32 [512], P(('groups', 'blk')), parts along dimension 0
- grad_w: float32 [1536, 128], P(('groups', 'blk')), parts along dimension 0
There are 2 independent parts, one for each index of `groups`. A program takes and returns all parts, laid end to end along the dimension named above; an argument that names none is the same for every part. Nothing has to cross between parts.
Inputs may be any that keep to these rules, and one draw needn't show every extreme that they name: A permutation: the teacher scores of query q are stored as row teacher_pos[q] of teacher_rows.
All inputs are finite; a program needn't handle non-finite values.
Results may differ from a plain program's by a relative error of at most 0.0073.
Values may be sent and summed in bfloat16 or wider, within the bound.
A program may use at most 128 MiB of HBM per device.

v0:
```python
import jax
import jax.numpy as jnp
from jax import lax
from jax.sharding import PartitionSpec as P

CYCLE = 4


smoothing_heat_factor = 0.05
epsilon = 1e-06


def shifted(value, axis, steps):
    count = lax.axis_size(axis)
    pairs = [(source, (source + steps) % count) for source in range(count)]
    return lax.ppermute(value, axis, pairs)


def normalize(raw):
    length = jnp.sqrt(jnp.sum(raw * raw, axis=1, keepdims=True) + epsilon)
    return (raw / length, length)


def token_terms(query_flat, passage_flat, lengths):
    count = lengths.shape[0]
    token_affinity_table = lax.dot_general(
        query_flat, passage_flat, (((1,), (1,)), ((), ())), preferred_element_type=jnp.float32
    )
    token_affinity_table = token_affinity_table.reshape(query_flat.shape[0], count, -1)
    pairwise_dot_entries = (
        jnp.arange(token_affinity_table.shape[2], dtype=jnp.int32)[None, :] < lengths[:, None]
    )
    natural_power_entries = jnp.where(
        pairwise_dot_entries[None], jnp.exp(token_affinity_table / smoothing_heat_factor), 0.0
    )
    return (natural_power_entries, jnp.sum(natural_power_entries, axis=2))


def soft_scores(query_flat, passage_flat, lengths, query_matrix):
    natural_power_entries, power_totals_row = token_terms(query_flat, passage_flat, lengths)
    smooth_peak_values = smoothing_heat_factor * jnp.log(power_totals_row)
    return jnp.sum(smooth_peak_values.reshape(query_matrix, -1, lengths.shape[0]), axis=1)


def score_grads(query_flat, passage_flat, lengths, score_grad):
    natural_power_entries, power_totals_row = token_terms(query_flat, passage_flat, lengths)
    rows = query_flat.shape[0]
    query_matrix, count = score_grad.shape
    scale = (score_grad[:, None, :] / power_totals_row.reshape(query_matrix, -1, count)).reshape(
        rows, count
    )
    weights = (natural_power_entries * scale[:, :, None]).reshape(rows, -1).astype(jnp.bfloat16)
    query_grad = jnp.dot(weights, passage_flat, preferred_element_type=jnp.float32)
    passage_grad = lax.dot_general(
        weights, query_flat, (((0,), (0,)), ((), ())), preferred_element_type=jnp.float32
    )
    return (query_grad, passage_grad)


def kl_terms(student, teacher, counts):
    valid = jnp.arange(student.shape[1], dtype=jnp.int32)[None, :] < counts[:, None]
    student_exp = jnp.where(valid, jnp.exp(student), 0.0)
    student_total = jnp.sum(student_exp, axis=1, keepdims=True)
    teacher_exp = jnp.where(valid, jnp.exp(teacher), 0.0)
    teacher_total = jnp.sum(teacher_exp, axis=1, keepdims=True)
    student_prob = student_exp / student_total
    teacher_prob = teacher_exp / teacher_total
    gap = teacher - jnp.log(teacher_total) - (student - jnp.log(student_total))
    loss = jnp.sum(jnp.where(valid, teacher_prob * gap, 0.0), axis=1)
    return (loss, student_prob - teacher_prob)


def raw_grad(unit, length, grad):
    return ((grad - unit * jnp.sum(unit * grad, axis=1, keepdims=True)) / length).astype(
        jnp.bfloat16
    )


def per_device(
    query_hidden, passage_hidden, projection, teacher_rows, teacher_pos, neg_count, pass_len
):
    query_matrix = query_hidden.shape[0]
    query_tokens = query_hidden.shape[1]
    width = query_hidden.shape[2]
    passages = passage_hidden.shape[0]
    passage_tokens = passage_hidden.shape[1]
    query_flat = query_hidden.reshape(query_matrix * query_tokens, width)
    passage_flat = passage_hidden.reshape(passages * passage_tokens, width)
    query_unit, query_length = normalize(
        jnp.dot(query_flat, projection, preferred_element_type=jnp.float32)
    )
    passage_unit, passage_length = normalize(
        jnp.dot(passage_flat, projection, preferred_element_type=jnp.float32)
    )
    query_outgoing = query_unit.astype(jnp.bfloat16)
    passage_send = passage_unit.astype(jnp.bfloat16)
    stored = lax.all_gather(teacher_rows, "blk", axis=0, tiled=True)
    teacher = jnp.take(stored, teacher_pos, axis=0)
    score_parts = []
    held = []
    current = query_outgoing
    for offset in range(CYCLE):
        if offset > 0:
            current = shifted(current, "blk", 1)
        held.append(current)
        scored = soft_scores(current, passage_send, pass_len, query_matrix)
        if offset > 0:
            scored = shifted(scored, "blk", -offset)
        score_parts.append(scored)
    student = jnp.concatenate(score_parts, axis=1)
    loss, score_grad = kl_terms(student, teacher, neg_count)
    query_total = jnp.zeros(query_unit.shape, jnp.float32)
    passage_total = jnp.zeros(passage_unit.shape, jnp.float32)
    for offset in range(CYCLE):
        portion_derivative = score_grad[:, offset * passages : (offset + 1) * passages]
        if offset > 0:
            portion_derivative = shifted(portion_derivative, "blk", offset)
        query_part, passage_part = score_grads(
            held[offset], passage_send, pass_len, portion_derivative
        )
        passage_total = passage_total + passage_part
        if offset > 0:
            query_part = shifted(query_part, "blk", -offset)
        query_total = query_total + query_part
    query_raw = raw_grad(query_unit, query_length, query_total)
    document_unprojected = raw_grad(passage_unit, passage_length, passage_total)
    contract = (((0,), (0,)), ((), ()))
    term = lax.dot_general(query_flat, query_raw, contract, preferred_element_type=jnp.float32)
    grad_w = lax.psum_scatter(
        term
        + lax.dot_general(
            passage_flat, document_unprojected, contract, preferred_element_type=jnp.float32
        ),
        "blk",
        scatter_dimension=0,
        tiled=True,
    )
    return (loss, grad_w)


def solution(mesh):
    return jax.shard_map(
        per_device,
        mesh=mesh,
        in_specs=(
            P(("groups", "blk"), None, None),
            P(("groups", "blk"), None, None),
            P(),
            P(("groups", "blk"), None),
            P(("groups", "blk")),
            P(("groups", "blk")),
            P(("groups", "blk")),
        ),
        out_specs=(P(("groups", "blk")), P(("groups", "blk"), None)),
        check_vma=False,
    )
```

profile of v0, /device:TPU:0, one launch (start us, length us, event | category | flops | bytes accessed | tf_op | source)
XLA Modules:
  0.0 242.0 jit_solution(9073984573945769077)
XLA Ops:
  14.1 3.4 %copy.26 = bf16[8,180,768]{2,1,0:T(8,128)(2,1)} copy(bf16[8,180,768]{2,0,1:T(8,128)(2,1)} %param.8) | data formatting | bytes 4423680 | tf_op args[1]
  17.5 2.6 %reshape.162 = bf16[1440,768]{1,0:T(8,128)(2,1)S(1)} reshape(bf16[8,180,768]{2,1,0:T(8,128)(2,1)} %copy.26) | data formatting | bytes 4423680 | tf_op jit(solution)/shard_map/reshape | solution.py:88
  22.1 2.1 fusion
  24.5 3.1 %exp.40 = f32[512,8,180]{0,2,1:T(8,128)} reshape(f32[512,1440]{0,1:T(8,128)} %fusion) | data formatting | bytes 5898240 | tf_op jit(solution)/shard_map/exp | solution.py:34
  27.6 24.4 %all_gather.3 = f32[256,32]{1,0:T(8,128)} all-gather(f32[16,32]{1,0:T(8,128)S(1)} %copy-done.11), channel_id=1, replica_groups=mesh['groups'=2,'blk'=16] {'blk'}, dimensions={0}, use_global_device_ids=true | all-gather | bytes 34816 | tf_op jit(solution)/shard_map/all_gather | solution.py:97
  52.9 3.1 %fusion.1 = f32[512,1440]{0,1:T(8,128)} fusion(bf16[1440,128]{1,0:T(8,128)(2,1)S(1)} %fusion.16, bf16[512,128]{0,1:T(8,128)(2,1)} %collective-permute-done), kind=kOutput, calls=%fused_computation.6 | convolution fusion | flops 189480960 | bytes 3448832 | tf_op jit(solution)/shard_map/dot_general | solution.py:26
  55.9 3.1 %exp.42 = f32[512,8,180]{0,2,1:T(8,128)} reshape(f32[512,1440]{0,1:T(8,128)} %fusion.1) | data formatting | bytes 5898240 | tf_op jit(solution)/shard_map/exp | solution.py:34
  59.9 3.1 %fusion.2 = f32[512,1440]{0,1:T(8,128)} fusion(bf16[1440,128]{1,0:T(8,128)(2,1)S(1)} %fusion.16, bf16[512,128]{0,1:T(8,128)(2,1)} %collective-permute-done.2), kind=kOutput, calls=%fused_computation.7 | convolution fusion | flops 189480960 | bytes 3448832 | tf_op jit(solution)/shard_map/dot_general | solution.py:26
  63.0 3.2 %exp.44 = f32[512,8,180]{0,2,1:T(8,128)} reshape(f32[512,1440]{0,1:T(8,128)} %fusion.2) | data formatting | bytes 5898240 | tf_op jit(solution)/shard_map/exp | solution.py:34
  67.3 3.0 %fusion.3 = f32[512,1440]{0,1:T(8,128)} fusion(bf16[1440,128]{1,0:T(8,128)(2,1)S(1)} %fusion.16, bf16[512,128]{0,1:T(8,128)(2,1)} %collective-permute-done.4), kind=kOutput, calls=%fused_computation.8 | convolution fusion | flops 189480960 | bytes 3448832 | tf_op jit(solution)/shard_map/dot_general | solution.py:26
  70.4 3.1 %exp.46 = f32[512,8,180]{0,2,1:T(8,128)} reshape(f32[512,1440]{0,1:T(8,128)} %fusion.3) | data formatting | bytes 5898240 | tf_op jit(solution)/shard_map/exp | solution.py:34
  73.5 5.7 %select_reduce_fusion.3 = (f32[512,8]{0,1:T(8,128)}, f32[512,8]{0,1:T(8,128)S(1)}, f32[512,8]{0,1:T(8,128)S(1)}, f32[512,8]{0,1:T(8,128)S(1)}) fusion(f32[512,8,180]{0,2,1:T(8,128)} %exp.40, pred[8,180]{1,0:T(8,128)(4,1)} %iota_compare_fusion, f32[512,8,180]{0,2,1:T(8,128)} %exp.42, f32[512,8,180]{0,2,1:T(8,128)} %exp.44, f32[512,8,180]{0,2,1:T(8,128)} %exp.46), kind=kLoop, calls=%fused_computation.12 | loop fusion | flops 5881856 | bytes 11863456 | tf_op jit(solution)/shard_map/reduce_sum | solution.py:36
  89.8 3.4 %collective-permute-start.1 = (f32[16,8]{1,0:T(8,128)}, f32[16,8]{1,0:T(8,128)}, u32[]{:S(2)}, u32[]{:S(2)}) collective-permute-start(f32[16,8]{1,0:T(8,128)} %copy.27), channel_id=1, source_target_pairs={{0,15},{1,0},{2,1},{3,2},{4,3},{5,4},{6,5},{7,6},{8,7},{9,8},{10,9... | collective-permute-start | bytes 1544 | tf_op jit(solution)/shard_map/ppermute | solution.py:16
  110.4 3.5 %collective-permute-start.10 = (f32[16,8]{1,0:T(8,128)}, f32[16,8]{1,0:T(8,128)}, u32[]{:S(2)}, u32[]{:S(2)}) collective-permute-start(f32[16,8]{1,0:T(8,128)} %get-tuple-element.17), channel_id=1, source_target_pairs={{0,3},{1,4},{2,5},{3,6},{4,7},{5,8},{6,9},{7,10},{8,11},{9,12},{10... | collective-permute-start | bytes 1544 | tf_op jit(solution)/shard_map/ppermute | solution.py:16
  119.5 3.1 %mul.115 = f32[512,1440]{0,1:T(8,128)} reshape(f32[512,8,180]{0,2,1:T(8,128)} %mul.114) | data formatting | bytes 5898240 | tf_op jit(solution)/shard_map/mul | solution.py:52
  136.4 3.1 %mul.124 = f32[512,1440]{0,1:T(8,128)} reshape(f32[512,8,180]{0,2,1:T(8,128)} %mul.123) | data formatting | bytes 5898240 | tf_op jit(solution)/shard_map/mul | solution.py:52
  141.5 3.1 %mul.121 = f32[512,1440]{0,1:T(8,128)} reshape(f32[512,8,180]{0,2,1:T(8,128)} %mul.120) | data formatting | bytes 5898240 | tf_op jit(solution)/shard_map/mul | solution.py:52
  144.6 2.1 mul.117
  146.7 3.1 %mul.118 = f32[512,1440]{0,1:T(8,128)} reshape(f32[512,8,180]{0,2,1:T(8,128)} %mul.117) | data formatting | bytes 5898240 | tf_op jit(solution)/shard_map/mul | solution.py:52
  149.8 8.6 %multiply_convert_fusion = (bf16[512,1440]{0,1:T(8,128)(2,1)S(1)}, bf16[512,1440]{0,1:T(8,128)(2,1)S(1)}, bf16[512,1440]{0,1:T(8,128)(2,1)S(1)}, bf16[512,1440]{0,1:T(8,128)(2,1)S(1)}) fusion(f32[512,1440]{0,1:T(8,128)} %mul.124, f32[512,1440]{0,1:T(8,128)} %fusion.3, pred[1440]{0:T(1024)(128)(4,1)S(1)} %copy-done.12, f32[512,1440]{0,1:T(8,128)} %mul.118, ...), kind=kLoop, calls=%fused_computation.13 | loop fusion | flops 8847360 | bytes 29492640 | tf_op jit(solution)/shard_map/convert_element_type | solution.py:52
  159.7 4.8 %collective-permute-start.9 = (f32[512,128]{0,1:T(8,128)S(1)}, f32[512,128]{0,1:T(8,128)S(1)}, u32[]{:S(2)}, u32[]{:S(2)}) collective-permute-start(f32[512,128]{0,1:T(8,128)S(1)} %fusion.19), channel_id=1, source_target_pairs={{0,14},{1,15},{2,0},{3,1},{4,2},{5,3},{6,4},{7,5},{8,6},{9,7},{10,... | collective-permute-start | bytes 786440 | tf_op jit(solution)/shard_map/ppermute | solution.py:16
  171.2 3.2 %collective-permute-done.7 = f32[512,128]{0,1:T(8,128)S(1)} collective-permute-done((f32[512,128]{0,1:T(8,128)S(1)}, f32[512,128]{0,1:T(8,128)S(1)}, u32[]{:S(2)}, u32[]{:S(2)}) %collective-permute-start.7) | collective-permute-done | bytes 262176 | tf_op jit(solution)/shard_map/ppermute | solution.py:16
  174.5 2.8 %collective-permute-done.11 = f32[512,128]{0,1:T(8,128)S(1)} collective-permute-done((f32[512,128]{0,1:T(8,128)S(1)}, f32[512,128]{0,1:T(8,128)S(1)}, u32[]{:S(2)}, u32[]{:S(2)}) %collective-permute-start.11) | collective-permute-done | bytes 262176 | tf_op jit(solution)/shard_map/ppermute | solution.py:16
  179.0 56.2 %reduce-scatter.4.cloned.1.call-done = f32[48,128]{1,0:T(8,128)} async-done(((f32[768,128]{1,0:T(8,128)}), f32[48,128]{1,0:T(8,128)}) %reduce-scatter.4.cloned.1.call-update) | async-done | bytes 24592
  (114 shorter events, 70.6 us)
Async XLA Ops:
  7.2 1.1 copy-start
  7.2 228.0 %reduce-scatter.4.cloned.1.call-start = ((), (), s32[]{:S(2)}) async-start(), calls=%async_computation.1 | async-start | bytes 417792
  10.4 42.2 %collective-permute-start = (bf16[512,128]{0,1:T(8,128)(2,1)S(1)}, bf16[512,128]{0,1:T(8,128)(2,1)}, u32[]{:S(2)}, u32[]{:S(2)}) collective-permute-start(bf16[512,128]{0,1:T(8,128)(2,1)S(1)} %fusion.15), channel_id=1, source_target_pairs={{0,1},{1,2},{2,3},{3,4},{4,5},{5,6},{6,7},{7,8},{8,9},{9,10},{10,1... | collective-permute-start | bytes 393224 | tf_op jit(solution)/shard_map/ppermute | solution.py:16
  17.5 2.6 %copy-start.5 = (bf16[768,128]{1,0:T(8,128)(2,1)S(1)}, bf16[768,128]{1,0:T(8,128)(2,1)}, u32[]{:S(2)}) copy-start(bf16[768,128]{1,0:T(8,128)(2,1)} %param.9) | copy-start | bytes 589828
  21.0 3.3 %copy-start.13 = (s32[8]{0:T(128)S(1)}, s32[8]{0:T(128)}, u32[]{:S(2)}) copy-start(s32[8]{0:T(128)} %param.13) | copy-start | bytes 100
  21.0 1.1 copy-start.7
  24.4 3.1 %copy-start.11 = (f32[16,32]{1,0:T(8,128)S(1)}, f32[16,32]{1,0:T(8,128)}, u32[]{:S(2)}) copy-start(f32[16,32]{1,0:T(8,128)} %param.10) | copy-start | bytes 6148
  52.5 7.4 %collective-permute-start.2 = (bf16[512,128]{0,1:T(8,128)(2,1)}, bf16[512,128]{0,1:T(8,128)(2,1)}, u32[]{:S(2)}, u32[]{:S(2)}) collective-permute-start(bf16[512,128]{0,1:T(8,128)(2,1)} %collective-permute-done), channel_id=1, source_target_pairs={{0,1},{1,2},{2,3},{3,4},{4,5},{5,6},{6,7},{7,8},{8,9},{9,10},{10,1... | collective-permute-start | bytes 393224 | tf_op jit(solution)/shard_map/ppermute | solution.py:16
  59.9 7.4 %collective-permute-start.4 = (bf16[512,128]{0,1:T(8,128)(2,1)}, bf16[512,128]{0,1:T(8,128)(2,1)}, u32[]{:S(2)}, u32[]{:S(2)}) collective-permute-start(bf16[512,128]{0,1:T(8,128)(2,1)} %collective-permute-done.2), channel_id=1, source_target_pairs={{0,1},{1,2},{2,3},{3,4},{4,5},{5,6},{6,7},{7,8},{8,9},{9,10},{10,1... | collective-permute-start | bytes 393224 | tf_op jit(solution)/shard_map/ppermute | solution.py:16
  84.1 22.4 %collective-permute-start.5 = (f32[16,8]{1,0:T(8,128)}, f32[16,8]{1,0:T(8,128)}, u32[]{:S(2)}, u32[]{:S(2)}) collective-permute-start(f32[16,8]{1,0:T(8,128)} %copy.29), channel_id=1, source_target_pairs={{0,13},{1,14},{2,15},{3,0},{4,1},{5,2},{6,3},{7,4},{8,5},{9,6},{10... | collective-permute-start | bytes 1544 | tf_op jit(solution)/shard_map/ppermute | solution.py:16
  89.8 16.8 %collective-permute-start.1 = (f32[16,8]{1,0:T(8,128)}, f32[16,8]{1,0:T(8,128)}, u32[]{:S(2)}, u32[]{:S(2)}) collective-permute-start(f32[16,8]{1,0:T(8,128)} %copy.27), channel_id=1, source_target_pairs={{0,15},{1,0},{2,1},{3,2},{4,3},{5,4},{6,5},{7,6},{8,7},{9,8},{10,9... | collective-permute-start | bytes 1544 | tf_op jit(solution)/shard_map/ppermute | solution.py:16
  97.4 9.1 %collective-permute-start.3 = (f32[16,8]{1,0:T(8,128)}, f32[16,8]{1,0:T(8,128)}, u32[]{:S(2)}, u32[]{:S(2)}) collective-permute-start(f32[16,8]{1,0:T(8,128)} %copy.28), channel_id=1, source_target_pairs={{0,14},{1,15},{2,0},{3,1},{4,2},{5,3},{6,4},{7,5},{8,6},{9,7},{10,... | collective-permute-start | bytes 1544 | tf_op jit(solution)/shard_map/ppermute | solution.py:16
  109.6 13.0 %collective-permute-start.6 = (f32[16,8]{1,0:T(8,128)}, f32[16,8]{1,0:T(8,128)}, u32[]{:S(2)}, u32[]{:S(2)}) collective-permute-start(f32[16,8]{1,0:T(8,128)} %get-tuple-element.19), channel_id=1, source_target_pairs={{0,1},{1,2},{2,3},{3,4},{4,5},{5,6},{6,7},{7,8},{8,9},{9,10},{10,1... | collective-permute-start | bytes 1544 | tf_op jit(solution)/shard_map/ppermute | solution.py:16
  110.4 20.3 %collective-permute-start.10 = (f32[16,8]{1,0:T(8,128)}, f32[16,8]{1,0:T(8,128)}, u32[]{:S(2)}, u32[]{:S(2)}) collective-permute-start(f32[16,8]{1,0:T(8,128)} %get-tuple-element.17), channel_id=1, source_target_pairs={{0,3},{1,4},{2,5},{3,6},{4,7},{5,8},{6,9},{7,10},{8,11},{9,12},{10... | collective-permute-start | bytes 1544 | tf_op jit(solution)/shard_map/ppermute | solution.py:16
  113.8 13.1 %collective-permute-start.8 = (f32[16,8]{1,0:T(8,128)}, f32[16,8]{1,0:T(8,128)}, u32[]{:S(2)}, u32[]{:S(2)}) collective-permute-start(f32[16,8]{1,0:T(8,128)} %get-tuple-element.18), channel_id=1, source_target_pairs={{0,2},{1,3},{2,4},{3,5},{4,6},{5,7},{6,8},{7,9},{8,10},{9,11},{10,... | collective-permute-start | bytes 1544 | tf_op jit(solution)/shard_map/ppermute | solution.py:16
  141.5 3.1 %copy-start.6 = (f32[512,8]{0,1:T(8,128)S(1)}, f32[512,8]{0,1:T(8,128)}, u32[]{:S(2)}) copy-start(f32[512,8]{0,1:T(8,128)} %div.133) | copy-start | bytes 49156
  146.7 3.1 %copy-start.12 = (pred[1440]{0:T(1024)(128)(4,1)S(1)}, pred[1440]{0:T(1024)(128)(4,1)}, u32[]{:S(2)}) copy-start(pred[1440]{0:T(1024)(128)(4,1)} %lt.42) | copy-start | bytes 4324
  159.7 11.6 %collective-permute-start.9 = (f32[512,128]{0,1:T(8,128)S(1)}, f32[512,128]{0,1:T(8,128)S(1)}, u32[]{:S(2)}, u32[]{:S(2)}) collective-permute-start(f32[512,128]{0,1:T(8,128)S(1)} %fusion.19), channel_id=1, source_target_pairs={{0,14},{1,15},{2,0},{3,1},{4,2},{5,3},{6,4},{7,5},{8,6},{9,7},{10,... | collective-permute-start | bytes 786440 | tf_op jit(solution)/shard_map/ppermute | solution.py:16
  164.5 10.0 %collective-permute-start.7 = (f32[512,128]{0,1:T(8,128)S(1)}, f32[512,128]{0,1:T(8,128)S(1)}, u32[]{:S(2)}, u32[]{:S(2)}) collective-permute-start(f32[512,128]{0,1:T(8,128)S(1)} %fusion.18), channel_id=1, source_target_pairs={{0,15},{1,0},{2,1},{3,2},{4,3},{5,4},{6,5},{7,6},{8,7},{9,8},{10,9... | collective-permute-start | bytes 786440 | tf_op jit(solution)/shard_map/ppermute | solution.py:16
  164.5 12.8 %collective-permute-start.11 = (f32[512,128]{0,1:T(8,128)S(1)}, f32[512,128]{0,1:T(8,128)S(1)}, u32[]{:S(2)}, u32[]{:S(2)}) collective-permute-start(f32[512,128]{0,1:T(8,128)S(1)} %fusion.20), channel_id=1, source_target_pairs={{0,13},{1,14},{2,15},{3,0},{4,1},{5,2},{6,3},{7,4},{8,5},{9,6},{10... | collective-permute-start | bytes 786440 | tf_op jit(solution)/shard_map/ppermute | solution.py:16
  165.0 3.0 %copy-start.2 = (f32[1440,128]{1,0:T(8,128)S(1)}, f32[1440,128]{1,0:T(8,128)}, u32[]{:S(2)}) copy-start(f32[1440,128]{1,0:T(8,128)} %copy-done.1) | copy-start | bytes 2211844
  165.0 3.0 %copy-start.8 = (f32[1440]{0:T(1024)S(1)}, f32[1440]{0:T(1024)}, u32[]{:S(2)}) copy-start(f32[1440]{0:T(1024)} %copy-done.7) | copy-start | bytes 17284
  169.6 7.7 %copy-start.4 = (f32[512,128]{0,1:T(8,128)S(1)}, f32[512,128]{0,1:T(8,128)}, u32[]{:S(2)}) copy-start(f32[512,128]{0,1:T(8,128)} %copy-done.3) | copy-start | bytes 786436
  169.6 7.7 %copy-start.10 = (f32[512]{0:T(512)S(1)}, f32[512]{0:T(512)}, u32[]{:S(2)}) copy-start(f32[512]{0:T(512)} %copy-done.9) | copy-start | bytes 6148
  (3 other events, 2.3 us)
Sparse Core Ops, SparseCore 0:
  179.1 56.0 reduce-scatter.3
where the time goes:
time: 244 us; the launch traced here: 242 us
  local copies, waits for them, and re-layouts  70.7 us (29%)
  waiting for transfers between devices  64.7 us (27%)
  other arithmetic  33.5 us (14%)
  blocking collectives  24.4 us (10%)
  matrix products  21.7 us (9%)
  between operations  14.3 us (6%)
  starting transfers between devices  12.6 us (5%)
    unnamed x2, waiting for transfers between devices  56.2 us
    all_gather x1, blocking collectives, per_device(): stored = lax.all_gather(teacher_rows, 'blk', axis=0, tiled=True)  24.4 us
    mul x8, local copies, waits for them, and re-layouts, score_grads(): natural_power_entries * scale[:, :, None]  20.6 us
    exp x4, local copies, waits for them, and re-layouts, token_terms(): jnp.exp(token_affinity_table / smoothing_heat_factor)  12.6 us
    ppermute x12, starting transfers between devices, shifted(): return lax.ppermute(value, axis, pairs)  12.6 us
    dot_general x4, matrix products, token_terms(): lax.dot_general(query_flat, passage_flat, (((1,), (1,)), ((), ())), prefe...  11.3 us
    div x8, local copies, waits for them, and re-layouts, score_grads(): score_grad[:, None, :] / power_totals_row.reshape(query_matrix, -1, count)  9.58 us
    convert_element_type x1, other arithmetic, score_grads(): (natural_power_entries * scale[:, :, None]).reshape(rows, -1)  8.56 us
  transfers between devices with their start and end apart: 13, of which 6 were waited for; matrix products, arithmetic and copies ran while one was open for 30% of the time, Pallas kernels for 0%

commit v1 on v0

v1 whole, which is shorter than its diff:
```python
import functools
import math

import jax
import jax.numpy as jnp
from jax import lax
from jax.experimental import pallas as pl
from jax.experimental.pallas import tpu as pltpu
from jax.sharding import PartitionSpec as P

CYCLE = 4
HEAT = 0.05
EPSILON = 1e-06
EXP2_SCALE = math.log2(math.e) / HEAT
NT = (((1,), (1,)), ((), ()))
TN = (((0,), (0,)), ((), ()))


def dot32(a, b, dims):
    return lax.dot_general(
        a, b, dims, precision=lax.Precision.HIGHEST, preferred_element_type=jnp.float32
    )


def kernel(
    n, link_dtype,
    qh_ref, ph_ref, proj_ref, rows_ref, pos_ref, cnt_ref, len_ref,
    loss_ref, grad_ref,
    teach_own, teach_all, qraw, q_all, pv, plen, pu, exps, den, w_buf, pgrad,
    s_send, s_recv, g_send, g_recv, qg_send, qg_recv, part, part_own, part_recv,
    teach_ss, teach_rs, q_ss, q_rs, s_ss, s_rs, g_ss, g_rs, qg_ss, qg_rs, part_ss, part_rs,
):
    me = lax.axis_index("blk")
    queries, q_tokens, width = qh_ref.shape
    passages, p_tokens, _ = ph_ref.shape
    dim = proj_ref.shape[1]
    q_rows = queries * q_tokens
    padded = pu.shape[0] // passages

    def peer(shift):
        return lax.rem(me + shift + n, n)

    def remote(src, dst, ss, rs, target):
        return pltpu.make_async_remote_copy(
            src_ref=src, dst_ref=dst, send_sem=ss, recv_sem=rs,
            device_id={"blk": target}, device_id_type=pl.DeviceIdType.MESH,
        )

    barrier = pltpu.get_barrier_semaphore()

    @pl.loop(1, n)
    def _(k):
        pl.semaphore_signal(
            barrier, inc=1, device_id={"blk": peer(k)}, device_id_type=pl.DeviceIdType.MESH
        )

    projection = proj_ref[...]
    q_hidden = qh_ref[...].reshape(q_rows, width)
    raw = jnp.dot(q_hidden, projection, preferred_element_type=jnp.float32)
    qraw[...] = raw
    q_len = jnp.sqrt(jnp.sum(raw * raw, axis=1, keepdims=True) + EPSILON)
    q_all[0] = (raw / q_len).astype(jnp.bfloat16)
    teach_own[...] = jnp.zeros(teach_own.shape, jnp.float32)
    teach_own[:, : rows_ref.shape[1]] = rows_ref[...]
    teach_all[me] = teach_own[...]
    pl.semaphore_wait(barrier, n - 1)

    def q_copy(o):
        return remote(q_all.at[0], q_all.at[o], q_ss.at[o], q_rs.at[o], peer(o))

    for o in range(1, CYCLE):
        q_copy(o).start()

    def teach_send(k):
        return remote(teach_own, teach_all.at[me], teach_ss.at[k], teach_rs.at[k], peer(k))

    def teach_recv(k):
        return remote(teach_own, teach_all.at[peer(-k)], teach_ss.at[k], teach_rs.at[k], peer(k))

    @pl.loop(1, n)
    def _(k):
        teach_send(k).start()

    pv[...] = jnp.zeros(pv.shape, jnp.float32)
    plen[...] = jnp.ones(plen.shape, jnp.float32)

    for p in range(passages):
        at = p * padded
        raw_p = jnp.dot(ph_ref[p], projection, preferred_element_type=jnp.float32)
        length = jnp.sqrt(jnp.sum(raw_p * raw_p, axis=1, keepdims=True) + EPSILON)
        pv[at : at + p_tokens] = raw_p / length
        plen[at : at + p_tokens] = jnp.broadcast_to(length, raw_p.shape)
    pu[...] = pv[...].astype(jnp.bfloat16)
    pgrad[...] = jnp.zeros(pgrad.shape, jnp.float32)

    low = lax.broadcasted_iota(jnp.int32, (queries, q_rows), 0) * q_tokens
    lane = lax.broadcasted_iota(jnp.int32, (queries, q_rows), 1)
    spread = jnp.where((lane >= low) & (lane < low + q_tokens), 1.0, 0.0)
    token = lax.broadcasted_iota(jnp.int32, (padded, q_rows), 0)

    s_send[...] = jnp.zeros(s_send.shape, jnp.float32)
    g_send[...] = jnp.zeros(g_send.shape, jnp.float32)

    def s_copy(o):
        return remote(s_send.at[o], s_recv.at[o], s_ss.at[o], s_rs.at[o], peer(-o))

    def g_copy(o):
        return remote(g_send.at[o], g_recv.at[o], g_ss.at[o], g_rs.at[o], peer(o))

    def qg_copy(o):
        return remote(qg_send.at[o], qg_recv.at[o], qg_ss.at[o], qg_rs.at[o], peer(-o))

    def score(o):
        units = q_all[o]

        @pl.loop(0, passages)
        def _(p):
            at = pl.ds(pl.multiple_of(p * padded, padded), padded)
            sims = lax.dot_general(pu[at], units, NT, preferred_element_type=jnp.float32)
            e = jnp.where(token < len_ref[0, p], jnp.exp2(sims * EXP2_SCALE), 0.0)
            exps[o, at] = e
            den[o, pl.ds(p, 1)] = jnp.sum(e, axis=0, keepdims=True)

        peaks = HEAT * jnp.log(den[o])
        return dot32(peaks, spread, NT)

    own_scores = score(0)
    for o in range(1, CYCLE):
        q_copy(o).wait_recv()
        s_send[o, :, :queries] = score(o)
        s_copy(o).start()

    @pl.loop(1, n)
    def _(k):
        teach_recv(k).wait_recv()

    stored = teach_all[...].reshape(n * queries, teach_all.shape[2])
    cand = CYCLE * passages
    rows = lax.broadcasted_iota(jnp.int32, (n * queries, queries), 0)
    pick = jnp.where(rows == pos_ref[...], 1.0, 0.0)
    teacher = dot32(jnp.transpose(stored)[:cand], pick, (((1,), (0,)), ((), ())))
    valid = lax.broadcasted_iota(jnp.int32, (cand, queries), 0) < cnt_ref[...]
    teacher_exp = jnp.where(valid, jnp.exp(teacher), 0.0)
    teacher_total = jnp.sum(teacher_exp, axis=0, keepdims=True)
    teacher_prob = teacher_exp / teacher_total
    teacher_log = teacher - jnp.log(teacher_total)

    student_parts = [own_scores]
    for o in range(1, CYCLE):
        s_copy(o).wait_recv()
        student_parts.append(s_recv[o, :, :queries])
    student = jnp.concatenate(student_parts, axis=0)
    student_exp = jnp.where(valid, jnp.exp(student), 0.0)
    student_total = jnp.sum(student_exp, axis=0, keepdims=True)
    score_grad = student_exp / student_total - teacher_prob
    for o in range(1, CYCLE):
        g_send[o, :, :queries] = score_grad[o * passages : (o + 1) * passages]
        g_copy(o).start()
    gap = teacher_log - (student - jnp.log(student_total))
    loss_ref[...] = jnp.sum(jnp.where(valid, teacher_prob * gap, 0.0), axis=0, keepdims=True)

    def backward(o, grads):
        units = q_all[o]
        den[o] = dot32(grads, spread, (((1,), (0,)), ((), ()))) / den[o]

        @pl.loop(0, passages)
        def _(p):
            at = pl.ds(pl.multiple_of(p * padded, padded), padded)
            w = (exps[o, at] * den[o, pl.ds(p, 1)]).astype(jnp.bfloat16)
            w_buf[at] = w
            pgrad[at] += jnp.dot(w, units, preferred_element_type=jnp.float32)

        return lax.dot_general(pu[...], w_buf[...], TN, preferred_element_type=jnp.float32)

    q_total = backward(0, score_grad[:passages])
    for o in range(1, CYCLE):
        g_copy(o).wait_recv()
        qg_send[o] = backward(o, g_recv[o, :, :queries]).astype(link_dtype)
        qg_copy(o).start()

    term = jnp.zeros((dim, width), jnp.float32)
    for p in range(passages):
        at = p * padded
        v = pv[at : at + p_tokens]
        g = pgrad[at : at + p_tokens]
        raw_g = (g - v * jnp.sum(v * g, axis=1, keepdims=True)) / plen[at : at + p_tokens]
        term = term + lax.dot_general(
            raw_g.astype(jnp.bfloat16), ph_ref[p], TN, preferred_element_type=jnp.float32
        )

    for o in range(1, CYCLE):
        qg_copy(o).wait_recv()
        q_total = q_total + qg_recv[o].astype(jnp.float32)
    g = jnp.transpose(q_total)
    raw = qraw[...]
    q_len = jnp.sqrt(jnp.sum(raw * raw, axis=1, keepdims=True) + EPSILON)
    v = raw / q_len
    raw_g = (g - v * jnp.sum(v * g, axis=1, keepdims=True)) / q_len
    term = term + lax.dot_general(
        raw_g.astype(jnp.bfloat16), qh_ref[...].reshape(q_rows, width), TN,
        preferred_element_type=jnp.float32,
    )
    whole = jnp.transpose(term)
    chunk = grad_ref.shape[0]
    for k in range(n):
        piece = whole[k * chunk : (k + 1) * chunk]
        part_own[k] = piece
        part[k] = piece.astype(link_dtype)

    def part_copy(k):
        return remote(part.at[peer(k)], part_recv.at[k], part_ss.at[k], part_rs.at[k], peer(k))

    @pl.loop(1, n)
    def _(k):
        part_copy(k).start()

    grad_ref[...] = part_own[me]

    @pl.loop(1, n)
    def _(k):
        part_copy(k).wait_recv()
        grad_ref[...] += part_recv[k].astype(jnp.float32)

    for o in range(1, CYCLE):
        q_copy(o).wait_send()
        s_copy(o).wait_send()
        g_copy(o).wait_send()
        qg_copy(o).wait_send()

    @pl.loop(1, n)
    def _(k):
        teach_send(k).wait_send()
        part_copy(k).wait_send()


def per_device(
    n, query_hidden, passage_hidden, projection, teacher_rows, teacher_pos, neg_count, pass_len
):
    queries, q_tokens, width = query_hidden.shape
    passages, p_tokens, _ = passage_hidden.shape
    dim = projection.shape[1]
    q_rows = queries * q_tokens
    padded = -(-p_tokens // 16) * 16
    p_rows = passages * padded
    chunk = width // n
    link_dtype = jnp.bfloat16
    f32, bf16 = jnp.float32, jnp.bfloat16
    vmem = pl.BlockSpec(memory_space=pltpu.VMEM)
    smem = pl.BlockSpec(memory_space=pltpu.SMEM)
    dma = pltpu.SemaphoreType.DMA
    loss, grad_w = pl.pallas_call(
        functools.partial(kernel, n, link_dtype),
        out_shape=(
            jax.ShapeDtypeStruct((1, queries), f32),
            jax.ShapeDtypeStruct((chunk, dim), f32),
        ),
        in_specs=[vmem] * 6 + [smem],
        out_specs=(vmem, vmem),
        scratch_shapes=[
            pltpu.VMEM((queries, 128), f32),
            pltpu.VMEM((n, queries, 128), f32),
            pltpu.VMEM((q_rows, dim), f32),
            pltpu.VMEM((CYCLE, q_rows, dim), bf16),
            pltpu.VMEM((p_rows, dim), f32),
            pltpu.VMEM((p_rows, dim), f32),
            pltpu.VMEM((p_rows, dim), bf16),
            pltpu.VMEM((CYCLE, p_rows, q_rows), f32),
            pltpu.VMEM((CYCLE, passages, q_rows), f32),
            pltpu.VMEM((p_rows, q_rows), bf16),
            pltpu.VMEM((p_rows, dim), f32),
            pltpu.VMEM((CYCLE, passages, 128), f32),
            pltpu.VMEM((CYCLE, passages, 128), f32),
            pltpu.VMEM((CYCLE, passages, 128), f32),
            pltpu.VMEM((CYCLE, passages, 128), f32),
            pltpu.VMEM((CYCLE, dim, q_rows), link_dtype),
            pltpu.VMEM((CYCLE, dim, q_rows), link_dtype),
            pltpu.VMEM((n, chunk, dim), link_dtype),
            pltpu.VMEM((n, chunk, dim), f32),
            pltpu.VMEM((n, chunk, dim), link_dtype),
            dma((n,)), dma((n,)),
            dma((CYCLE,)), dma((CYCLE,)),
            dma((CYCLE,)), dma((CYCLE,)),
            dma((CYCLE,)), dma((CYCLE,)),
            dma((CYCLE,)), dma((CYCLE,)),
            dma((n,)), dma((n,)),
        ],
        compiler_params=pltpu.CompilerParams(
            collective_id=0, has_side_effects=True, vmem_limit_bytes=50 * 1024 * 1024
        ),
    )(
        query_hidden,
        passage_hidden,
        projection,
        teacher_rows,
        teacher_pos.reshape(1, queries),
        neg_count.reshape(1, queries),
        pass_len.reshape(1, passages),
    )
    return (loss.reshape(queries), grad_w)


def solution(mesh):
    return jax.shard_map(
        functools.partial(per_device, mesh.shape["blk"]),
        mesh=mesh,
        in_specs=(
            P(("groups", "blk"), None, None),
            P(("groups", "blk"), None, None),
            P(),
            P(("groups", "blk"), None),
            P(("groups", "blk")),
            P(("groups", "blk")),
            P(("groups", "blk")),
        ),
        out_specs=(P(("groups", "blk")), P(("groups", "blk"), None)),
        check_vma=False,
    )
```

time: 244 us -> 45.4 us (0.19)
  local copies, waits for them, and re-layouts: 70.7 us -> 3.28 us
  waiting for transfers between devices: 64.7 us -> 0 us
  Pallas kernels: 0 us -> 41.2 us
  other arithmetic: 33.5 us -> 0 us
  blocking collectives: 24.4 us -> 0 us
  matrix products: 21.7 us -> 0 us
  between operations: 14.3 us -> 0.74 us
  starting transfers between devices: 12.6 us -> 0 us
    unnamed x2 -> x0, waiting for transfers between devices: 56.2 us -> none
    pallas_call x0 -> x1, Pallas kernels: none -> 41.2 us  [per_device(): pl.pallas_call(functools.partial(kernel, n, link_dtype), out_shape=(jax.S...]
    mul x12 -> x0, local copies, waits for them, and re-layouts: 26.3 us -> none  [the longest x8 20.6 us: score_grads(): natural_power_entries * scale[:, :, None]]
    all_gather x1 -> x0, blocking collectives: 24.4 us -> none  [per_device(): stored = lax.all_gather(teacher_rows, 'blk', axis=0, tiled=True)]
    dot_general x16 -> x0, matrix products: 21.7 us -> none  [the longest x4 11.3 us: token_terms(): lax.dot_general(query_flat, passage_flat, (((1,), (1,)), ((), ())), prefe...]
    reduce_sum x6 -> x0, other arithmetic: 12.7 us -> none  [the longest x4 6.1 us: soft_scores(): jnp.sum(smooth_peak_values.reshape(query_matrix, -1, lengths.shape[0]), a...]
    exp x4 -> x0, local copies, waits for them, and re-layouts: 12.6 us -> none  [token_terms(): jnp.exp(token_affinity_table / smoothing_heat_factor)]
    ppermute x12 -> x0, starting transfers between devices: 12.6 us -> none  [shifted(): return lax.ppermute(value, axis, pairs)]
  transfers between devices with their start and end apart: 13 -> 0, of which waited for: 6 -> 0; matrix products, arithmetic and copies ran while one was open for 30% -> 0% of each run, Pallas kernels for 0% -> 0%
where the time goes in v1:
time: 45.4 us; the launch traced here: 45.3 us
  Pallas kernels  41.2 us (91%)
  local copies, waits for them, and re-layouts  3.28 us (7%)
  between operations  0.74 us (2%)
    pallas_call x1, Pallas kernels, per_device(): pl.pallas_call(functools.partial(kernel, n, link_dtype), out_shape=(jax.S...  41.2 us
    unnamed x15, local copies, waits for them, and re-layouts  3.28 us

profile of v1, /device:TPU:0, one launch (start us, length us, event | category | flops | bytes accessed | tf_op | source)
XLA Modules:
  0.0 45.3 jit_solution(7694017962775195108)
XLA Ops:
  0.6 0.0 copy-start.5
  0.6 0.0 copy-start.4
  0.7 0.0 copy-start.3
  0.7 0.0 copy-start.2
  0.7 0.0 copy-start.1
  0.7 0.0 copy-start
  0.7 2.1 %copy.9.ph_ref = bf16[8,180,768]{2,1,0:T(8,128)(2,1)S(1)} copy(bf16[8,180,768]{2,0,1:T(8,128)(2,1)} %param.8) | data formatting | bytes 4423680 | tf_op args[1]
  2.8 0.0 copy-done.5
  2.8 0.0 copy-done.4
  2.8 0.0 copy-done.3
  2.9 0.0 copy-done.2
  2.9 0.0 copy-done.1
  2.9 0.0 copy-done
  2.9 41.2 %shard_map.86 = (f32[1,16]{1,0:T(1,128)S(1)}, f32[48,128]{1,0:T(8,128)S(1)}) custom-call(bf16[16,32,768]{2,1,0:T(8,128)(2,1)S(1)} %copy-done, bf16[8,180,768]{2,1,0:T(8,128)(2,1)S(1)} %copy.9.ph_ref, bf16[768,128]{1,0:T(8,128)(2,1)S(1)} %copy-done.1, f32[16,32]{1,0:T(8,128)S(1)} %copy-done.2, s32[1,16]{1,0:T(1,128)S(1)} %bitcast.4, s32[1,16]{1,0:T(1,128)S(1)} %bitcast.5, ...), custom_call_target="tpu_custom_call" | custom-call | tf_op jit(solution)/shard_map/pallas_call | solution.py:251
  44.1 0.5 %copy.12 = f32[16]{0:T(128)} copy(f32[16]{0:T(128)S(1)} %bitcast.7) | data formatting | bytes 128
  44.6 0.6 %copy.13 = f32[48,128]{1,0:T(8,128)} copy(f32[48,128]{1,0:T(8,128)S(1)} %get-tuple-element.9) | data formatting | bytes 49152
Async XLA Ops:
  0.6 2.2 %copy-start.5 = (s32[8]{0:T(128)S(1)}, s32[8]{0:T(128)}, u32[]{:S(2)}) copy-start(s32[8]{0:T(128)} %param.13) | copy-start | bytes 100
  0.6 2.2 %copy-start.4 = (s32[16]{0:T(128)S(1)}, s32[16]{0:T(128)}, u32[]{:S(2)}) copy-start(s32[16]{0:T(128)} %param.12) | copy-start | bytes 196
  0.7 2.2 %copy-start.3 = (s32[16]{0:T(128)S(1)}, s32[16]{0:T(128)}, u32[]{:S(2)}) copy-start(s32[16]{0:T(128)} %param.11) | copy-start | bytes 196
  0.7 2.2 %copy-start.2 = (f32[16,32]{1,0:T(8,128)S(1)}, f32[16,32]{1,0:T(8,128)}, u32[]{:S(2)}) copy-start(f32[16,32]{1,0:T(8,128)} %rows_ref.1) | copy-start | bytes 6148
  0.7 2.2 %copy-start.1 = (bf16[768,128]{1,0:T(8,128)(2,1)S(1)}, bf16[768,128]{1,0:T(8,128)(2,1)}, u32[]{:S(2)}) copy-start(bf16[768,128]{1,0:T(8,128)(2,1)} %proj_ref.1) | copy-start | bytes 589828
  0.7 2.2 %copy-start = (bf16[16,32,768]{2,1,0:T(8,128)(2,1)S(1)}, bf16[16,32,768]{2,1,0:T(8,128)(2,1)}, u32[]{:S(2)}) copy-start(bf16[16,32,768]{2,1,0:T(8,128)(2,1)} %qh_ref.1) | copy-start | bytes 2359300

commit v2 on v1

--- a/solution.py
+++ b/solution.py
@@ -26,16 +26,18 @@
     n, link_dtype,
     qh_ref, ph_ref, proj_ref, rows_ref, pos_ref, cnt_ref, len_ref,
     loss_ref, grad_ref,
-    teach_own, teach_all, qraw, q_all, pv, plen, pu, exps, den, w_buf, pgrad,
+    teach_own, teach_all, qraw, q_all, pv, plen, pu, put, exps, den, w_buf, pgrad,
     s_send, s_recv, g_send, g_recv, qg_send, qg_recv, part, part_own, part_recv,
     teach_ss, teach_rs, q_ss, q_rs, s_ss, s_rs, g_ss, g_rs, qg_ss, qg_rs, part_ss, part_rs,
 ):
     me = lax.axis_index("blk")
     queries, q_tokens, width = qh_ref.shape
-    passages, p_tokens, _ = ph_ref.shape
+    p_tokens, passages, _ = ph_ref.shape
     dim = proj_ref.shape[1]
     q_rows = queries * q_tokens
-    padded = pu.shape[0] // passages
+    p_rows = p_tokens * passages
+    step = next(t for t in (20, 12, 4, 2) if p_tokens % t == 0)
+    block = step * passages
 
     def peer(shift):
         return lax.rem(me + shift + n, n)
@@ -81,22 +83,23 @@
     def _(k):
         teach_send(k).start()
 
-    pv[...] = jnp.zeros(pv.shape, jnp.float32)
-    plen[...] = jnp.ones(plen.shape, jnp.float32)
-
-    for p in range(passages):
-        at = p * padded
-        raw_p = jnp.dot(ph_ref[p], projection, preferred_element_type=jnp.float32)
-        length = jnp.sqrt(jnp.sum(raw_p * raw_p, axis=1, keepdims=True) + EPSILON)
-        pv[at : at + p_tokens] = raw_p / length
-        plen[at : at + p_tokens] = jnp.broadcast_to(length, raw_p.shape)
-    pu[...] = pv[...].astype(jnp.bfloat16)
-    pgrad[...] = jnp.zeros(pgrad.shape, jnp.float32)
+    p_hidden = ph_ref[...].reshape(p_rows, width)
+    raw_p = jnp.dot(p_hidden, projection, preferred_element_type=jnp.float32)
+    length = jnp.sqrt(jnp.sum(raw_p * raw_p, axis=1, keepdims=True) + EPSILON)
+    units_p = raw_p / length
+    pv[...] = units_p
+    plen[...] = jnp.broadcast_to(length, raw_p.shape)
+    pu[...] = units_p.astype(jnp.bfloat16)
+    put[...] = jnp.transpose(units_p).astype(jnp.bfloat16)
 
     low = lax.broadcasted_iota(jnp.int32, (queries, q_rows), 0) * q_tokens
     lane = lax.broadcasted_iota(jnp.int32, (queries, q_rows), 1)
     spread = jnp.where((lane >= low) & (lane < low + q_tokens), 1.0, 0.0)
-    token = lax.broadcasted_iota(jnp.int32, (padded, q_rows), 0)
+    passage = lax.broadcasted_iota(jnp.int32, (passages, q_rows), 0)
+    limit = jnp.zeros((passages, q_rows), jnp.int32)
+    for p in range(passages):
+        limit = jnp.where(passage == p, len_ref[0, p], limit)
+    token = lax.broadcasted_iota(jnp.int32, (step, passages, q_rows), 0)
 
     s_send[...] = jnp.zeros(s_send.shape, jnp.float32)
     g_send[...] = jnp.zeros(g_send.shape, jnp.float32)
@@ -113,14 +116,17 @@
     def score(o):
         units = q_all[o]
 
-        @pl.loop(0, passages)
-        def _(p):
-            at = pl.ds(pl.multiple_of(p * padded, padded), padded)
+        def body(k, total):
+            at = pl.ds(pl.multiple_of(k * block, block), block)
             sims = lax.dot_general(pu[at], units, NT, preferred_element_type=jnp.float32)
-            e = jnp.where(token < len_ref[0, p], jnp.exp2(sims * EXP2_SCALE), 0.0)
-            exps[o, at] = e
-            den[o, pl.ds(p, 1)] = jnp.sum(e, axis=0, keepdims=True)
-
+            sims = sims.reshape(step, passages, q_rows)
+            e = jnp.where(token < (limit - k * step)[None], jnp.exp2(sims * EXP2_SCALE), 0.0)
+            exps[o, pl.ds(k * step, step)] = e
+            return total + jnp.sum(e, axis=0)
+
+        den[o] = lax.fori_loop(
+            0, p_tokens // step, body, jnp.zeros((passages, q_rows), jnp.float32)
+        )
         peaks = HEAT * jnp.log(den[o])
         return dot32(peaks, spread, NT)
 
@@ -161,16 +167,21 @@
 
     def backward(o, grads):
         units = q_all[o]
-        den[o] = dot32(grads, spread, (((1,), (0,)), ((), ()))) / den[o]
-
-        @pl.loop(0, passages)
-        def _(p):
-            at = pl.ds(pl.multiple_of(p * padded, padded), padded)
-            w = (exps[o, at] * den[o, pl.ds(p, 1)]).astype(jnp.bfloat16)
+        scale = dot32(grads, spread, (((1,), (0,)), ((), ()))) / den[o]
+
+        @pl.loop(0, p_tokens // step)
+        def _(k):
+            at = pl.ds(pl.multiple_of(k * block, block), block)
+            w = exps[o, pl.ds(k * step, step)] * scale[None]
+            w = w.reshape(block, q_rows).astype(jnp.bfloat16)
             w_buf[at] = w
-            pgrad[at] += jnp.dot(w, units, preferred_element_type=jnp.float32)
-
-        return lax.dot_general(pu[...], w_buf[...], TN, preferred_element_type=jnp.float32)
+            part_grad = jnp.dot(w, units, preferred_element_type=jnp.float32)
+            if o == 0:
+                pgrad[at] = part_grad
+            else:
+                pgrad[at] += part_grad
+
+        return jnp.dot(put[...], w_buf[...], preferred_element_type=jnp.float32)
 
     q_total = backward(0, score_grad[:passages])
     for o in range(1, CYCLE):
@@ -178,15 +189,13 @@
         qg_send[o] = backward(o, g_recv[o, :, :queries]).astype(link_dtype)
         qg_copy(o).start()
 
-    term = jnp.zeros((dim, width), jnp.float32)
-    for p in range(passages):
-        at = p * padded
-        v = pv[at : at + p_tokens]
-        g = pgrad[at : at + p_tokens]
-        raw_g = (g - v * jnp.sum(v * g, axis=1, keepdims=True)) / plen[at : at + p_tokens]
-        term = term + lax.dot_general(
-            raw_g.astype(jnp.bfloat16), ph_ref[p], TN, preferred_element_type=jnp.float32
-        )
+    v_p = pv[...]
+    g_p = pgrad[...]
+    raw_g = (g_p - v_p * jnp.sum(v_p * g_p, axis=1, keepdims=True)) / plen[...]
+    term = lax.dot_general(
+        raw_g.astype(jnp.bfloat16), ph_ref[...].reshape(p_rows, width), TN,
+        preferred_element_type=jnp.float32,
+    )
 
     for o in range(1, CYCLE):
         qg_copy(o).wait_recv()
@@ -240,8 +249,7 @@
     passages, p_tokens, _ = passage_hidden.shape
     dim = projection.shape[1]
     q_rows = queries * q_tokens
-    padded = -(-p_tokens // 16) * 16
-    p_rows = passages * padded
+    p_rows = passages * p_tokens
     chunk = width // n
     link_dtype = jnp.bfloat16
     f32, bf16 = jnp.float32, jnp.bfloat16
@@ -264,7 +272,8 @@
             pltpu.VMEM((p_rows, dim), f32),
             pltpu.VMEM((p_rows, dim), f32),
             pltpu.VMEM((p_rows, dim), bf16),
-            pltpu.VMEM((CYCLE, p_rows, q_rows), f32),
+            pltpu.VMEM((dim, p_rows), bf16),
+            pltpu.VMEM((CYCLE, p_tokens, passages, q_rows), f32),
             pltpu.VMEM((CYCLE, passages, q_rows), f32),
             pltpu.VMEM((p_rows, q_rows), bf16),
             pltpu.VMEM((p_rows, dim), f32),
@@ -289,7 +298,7 @@
         ),
     )(
         query_hidden,
-        passage_hidden,
+        jnp.transpose(passage_hidden, (1, 0, 2)),
         projection,
         teacher_rows,
         teacher_pos.reshape(1, queries),

time: 45.4 us -> 50.2 us (1.11)
  local copies, waits for them, and re-layouts: 3.28 us -> 7.46 us
  Pallas kernels: 41.2 us -> 41.8 us
    unnamed x15 -> x16, local copies, waits for them, and re-layouts: 3.28 us -> 7.46 us
    pallas_call x1, Pallas kernels: 41.2 us -> 41.8 us  [per_device(): pl.pallas_call(functools.partial(kernel, n, link_dtype), out_shape=(jax.S...]
where the time goes in v2:
time: 50.2 us; the launch traced here: 49.9 us
  Pallas kernels  41.8 us (83%)
  local copies, waits for them, and re-layouts  7.46 us (15%)
  between operations  0.66 us (1%)
    pallas_call x1, Pallas kernels, per_device(): pl.pallas_call(functools.partial(kernel, n, link_dtype), out_shape=(jax.S...  41.8 us
    unnamed x16, local copies, waits for them, and re-layouts  7.46 us

profile of v2, /device:TPU:0, one launch (start us, length us, event | category | flops | bytes accessed | tf_op | source)
XLA Modules:
  0.0 49.9 jit_solution(15395372702196335263)
XLA Ops:
  0.6 0.0 copy-start
  0.6 1.6 %copy-done = bf16[8,180,768]{2,0,1:T(8,128)(2,1)S(1)} copy-done((bf16[8,180,768]{2,0,1:T(8,128)(2,1)S(1)}, bf16[8,180,768]{2,0,1:T(8,128)(2,1)}, u32[]{:S(2)}) %copy-start) | copy-done | bytes 2211864
  2.3 0.0 copy-start.1
  2.3 1.1 %copy-done.1 = bf16[16,32,768]{2,1,0:T(8,128)(2,1)S(1)} copy-done((bf16[16,32,768]{2,1,0:T(8,128)(2,1)S(1)}, bf16[16,32,768]{2,1,0:T(8,128)(2,1)}, u32[]{:S(2)}) %copy-start.1) | copy-done | bytes 786456
  3.4 0.0 copy-start.2
  3.4 0.9 %copy-done.2 = bf16[768,128]{1,0:T(8,128)(2,1)S(1)} copy-done((bf16[768,128]{1,0:T(8,128)(2,1)S(1)}, bf16[768,128]{1,0:T(8,128)(2,1)}, u32[]{:S(2)}) %copy-start.2) | copy-done | bytes 196632
  4.3 0.0 copy-start.3
  4.3 0.7 %copy-done.3 = f32[16,32]{1,0:T(8,128)S(1)} copy-done((f32[16,32]{1,0:T(8,128)S(1)}, f32[16,32]{1,0:T(8,128)}, u32[]{:S(2)}) %copy-start.3) | copy-done | bytes 2072
  5.0 0.0 copy-start.4
  5.0 0.7 %copy-done.4 = s32[16]{0:T(128)S(1)} copy-done((s32[16]{0:T(128)S(1)}, s32[16]{0:T(128)}, u32[]{:S(2)}) %copy-start.4) | copy-done | bytes 88
  5.7 0.0 copy-start.5
  5.7 0.7 %copy-done.5 = s32[16]{0:T(128)S(1)} copy-done((s32[16]{0:T(128)S(1)}, s32[16]{0:T(128)}, u32[]{:S(2)}) %copy-start.5) | copy-done | bytes 88
  6.3 0.0 copy-start.6
  6.3 0.7 %copy-done.6 = s32[8]{0:T(128)S(1)} copy-done((s32[8]{0:T(128)S(1)}, s32[8]{0:T(128)}, u32[]{:S(2)}) %copy-start.6) | copy-done | bytes 56
  7.0 41.8 %shard_map.86 = (f32[1,16]{1,0:T(1,128)S(1)}, f32[48,128]{1,0:T(8,128)S(1)}) custom-call(bf16[16,32,768]{2,1,0:T(8,128)(2,1)S(1)} %copy-done.1, bf16[180,8,768]{2,1,0:T(8,128)(2,1)S(1)} %bitcast.5, bf16[768,128]{1,0:T(8,128)(2,1)S(1)} %copy-done.2, f32[16,32]{1,0:T(8,128)S(1)} %copy-done.3, s32[1,16]{1,0:T(1,128)S(1)} %bitcast.6, s32[1,16]{1,0:T(1,128)S(1)} %bitcast.7, ...), custom_call_target="tpu_custom_call" | custom-call | tf_op jit(solution)/shard_map/pallas_call | solution.py:259
  48.8 0.5 %copy.11 = f32[16]{0:T(128)} copy(f32[16]{0:T(128)S(1)} %bitcast.9) | data formatting | bytes 128
  49.3 0.6 %copy.12 = f32[48,128]{1,0:T(8,128)} copy(f32[48,128]{1,0:T(8,128)S(1)} %get-tuple-element.9) | data formatting | bytes 49152
Async XLA Ops:
  0.6 1.6 %copy-start = (bf16[8,180,768]{2,0,1:T(8,128)(2,1)S(1)}, bf16[8,180,768]{2,0,1:T(8,128)(2,1)}, u32[]{:S(2)}) copy-start(bf16[8,180,768]{2,0,1:T(8,128)(2,1)} %param.8) | copy-start | bytes 6635524
  2.3 1.1 %copy-start.1 = (bf16[16,32,768]{2,1,0:T(8,128)(2,1)S(1)}, bf16[16,32,768]{2,1,0:T(8,128)(2,1)}, u32[]{:S(2)}) copy-start(bf16[16,32,768]{2,1,0:T(8,128)(2,1)} %qh_ref.1) | copy-start | bytes 2359300
  3.4 0.9 %copy-start.2 = (bf16[768,128]{1,0:T(8,128)(2,1)S(1)}, bf16[768,128]{1,0:T(8,128)(2,1)}, u32[]{:S(2)}) copy-start(bf16[768,128]{1,0:T(8,128)(2,1)} %proj_ref.1) | copy-start | bytes 589828
  4.3 0.7 %copy-start.3 = (f32[16,32]{1,0:T(8,128)S(1)}, f32[16,32]{1,0:T(8,128)}, u32[]{:S(2)}) copy-start(f32[16,32]{1,0:T(8,128)} %rows_ref.1) | copy-start | bytes 6148
  5.0 0.7 %copy-start.4 = (s32[16]{0:T(128)S(1)}, s32[16]{0:T(128)}, u32[]{:S(2)}) copy-start(s32[16]{0:T(128)} %param.11) | copy-start | bytes 196
  5.7 0.7 %copy-start.5 = (s32[16]{0:T(128)S(1)}, s32[16]{0:T(128)}, u32[]{:S(2)}) copy-start(s32[16]{0:T(128)} %param.12) | copy-start | bytes 196
  6.3 0.7 %copy-start.6 = (s32[8]{0:T(128)S(1)}, s32[8]{0:T(128)}, u32[]{:S(2)}) copy-start(s32[8]{0:T(128)} %param.13) | copy-start | bytes 100

commit v3 on v2

--- a/solution.py
+++ b/solution.py
@@ -1,5 +1,4 @@
 import functools
-import math
 
 import jax
 import jax.numpy as jnp
@@ -11,7 +10,6 @@
 CYCLE = 4
 HEAT = 0.05
 EPSILON = 1e-06
-EXP2_SCALE = math.log2(math.e) / HEAT
 NT = (((1,), (1,)), ((), ()))
 TN = (((0,), (0,)), ((), ()))
 
@@ -32,12 +30,11 @@
 ):
     me = lax.axis_index("blk")
     queries, q_tokens, width = qh_ref.shape
-    p_tokens, passages, _ = ph_ref.shape
+    passages = len_ref.shape[1]
+    p_tokens = ph_ref.shape[0] // passages
     dim = proj_ref.shape[1]
     q_rows = queries * q_tokens
-    p_rows = p_tokens * passages
-    step = next(t for t in (20, 12, 4, 2) if p_tokens % t == 0)
-    block = step * passages
+    p_rows = ph_ref.shape[0]
 
     def peer(shift):
         return lax.rem(me + shift + n, n)
@@ -65,32 +62,31 @@
     teach_own[...] = jnp.zeros(teach_own.shape, jnp.float32)
     teach_own[:, : rows_ref.shape[1]] = rows_ref[...]
     teach_all[me] = teach_own[...]
-    pl.semaphore_wait(barrier, n - 1)
-
-    def q_copy(o):
-        return remote(q_all.at[0], q_all.at[o], q_ss.at[o], q_rs.at[o], peer(o))
-
-    for o in range(1, CYCLE):
-        q_copy(o).start()
-
-    def teach_send(k):
-        return remote(teach_own, teach_all.at[me], teach_ss.at[k], teach_rs.at[k], peer(k))
-
-    def teach_recv(k):
-        return remote(teach_own, teach_all.at[peer(-k)], teach_ss.at[k], teach_rs.at[k], peer(k))
-
-    @pl.loop(1, n)
-    def _(k):
-        teach_send(k).start()
-
-    p_hidden = ph_ref[...].reshape(p_rows, width)
-    raw_p = jnp.dot(p_hidden, projection, preferred_element_type=jnp.float32)
+    raw_p = jnp.dot(ph_ref[...], projection, preferred_element_type=jnp.float32)
     length = jnp.sqrt(jnp.sum(raw_p * raw_p, axis=1, keepdims=True) + EPSILON)
     units_p = raw_p / length
     pv[...] = units_p
     plen[...] = jnp.broadcast_to(length, raw_p.shape)
     pu[...] = units_p.astype(jnp.bfloat16)
     put[...] = jnp.transpose(units_p).astype(jnp.bfloat16)
+
+    pl.semaphore_wait(barrier, n - 1)
+
+    def q_copy(o):
+        return remote(q_all.at[0], q_all.at[o], q_ss.at[o], q_rs.at[o], peer(o))
+
+    for o in range(1, CYCLE):
+        q_copy(o).start()
+
+    def teach_send(k):
+        return remote(teach_own, teach_all.at[me], teach_ss.at[k], teach_rs.at[k], peer(k))
+
+    def teach_recv(k):
+        return remote(teach_own, teach_all.at[peer(-k)], teach_ss.at[k], teach_rs.at[k], peer(k))
+
+    @pl.loop(1, n)
+    def _(k):
+        teach_send(k).start()
 
     low = lax.broadcasted_iota(jnp.int32, (queries, q_rows), 0) * q_tokens
     lane = lax.broadcasted_iota(jnp.int32, (queries, q_rows), 1)
@@ -99,7 +95,6 @@
     limit = jnp.zeros((passages, q_rows), jnp.int32)
     for p in range(passages):
         limit = jnp.where(passage == p, len_ref[0, p], limit)
-    token = lax.broadcasted_iota(jnp.int32, (step, passages, q_rows), 0)
 
     s_send[...] = jnp.zeros(s_send.shape, jnp.float32)
     g_send[...] = jnp.zeros(g_send.shape, jnp.float32)
@@ -116,17 +111,14 @@
     def score(o):
         units = q_all[o]
 
-        def body(k, total):
-            at = pl.ds(pl.multiple_of(k * block, block), block)
-            sims = lax.dot_general(pu[at], units, NT, preferred_element_type=jnp.float32)
-            sims = sims.reshape(step, passages, q_rows)
-            e = jnp.where(token < (limit - k * step)[None], jnp.exp2(sims * EXP2_SCALE), 0.0)
-            exps[o, pl.ds(k * step, step)] = e
-            return total + jnp.sum(e, axis=0)
-
-        den[o] = lax.fori_loop(
-            0, p_tokens // step, body, jnp.zeros((passages, q_rows), jnp.float32)
-        )
+        sims = lax.dot_general(pu[...], units, NT, preferred_element_type=jnp.float32)
+        total = jnp.zeros((passages, q_rows), jnp.float32)
+        for t in range(p_tokens):
+            e = jnp.exp(sims[t * passages : (t + 1) * passages] * (1.0 / HEAT))
+            e = jnp.where(limit > t, e, 0.0)
+            exps[o, t] = e
+            total = total + e
+        den[o] = total
         peaks = HEAT * jnp.log(den[o])
         return dot32(peaks, spread, NT)
 
@@ -169,31 +161,29 @@
         units = q_all[o]
         scale = dot32(grads, spread, (((1,), (0,)), ((), ()))) / den[o]
 
-        @pl.loop(0, p_tokens // step)
-        def _(k):
-            at = pl.ds(pl.multiple_of(k * block, block), block)
-            w = exps[o, pl.ds(k * step, step)] * scale[None]
-            w = w.reshape(block, q_rows).astype(jnp.bfloat16)
-            w_buf[at] = w
-            part_grad = jnp.dot(w, units, preferred_element_type=jnp.float32)
-            if o == 0:
-                pgrad[at] = part_grad
-            else:
-                pgrad[at] += part_grad
-
-        return jnp.dot(put[...], w_buf[...], preferred_element_type=jnp.float32)
+        w = (exps[o] * scale[None]).reshape(p_rows, q_rows).astype(jnp.bfloat16)
+        w_buf[...] = w
+        q_grad = jnp.dot(put[...], w_buf[...], preferred_element_type=jnp.float32)
+        if o > 0:
+            qg_send[o] = q_grad.astype(link_dtype)
+            qg_copy(o).start()
+        part_grad = jnp.dot(w_buf[...], units, preferred_element_type=jnp.float32)
+        if o == 0:
+            pgrad[...] = part_grad
+        else:
+            pgrad[...] += part_grad
+        return q_grad
 
     q_total = backward(0, score_grad[:passages])
     for o in range(1, CYCLE):
         g_copy(o).wait_recv()
-        qg_send[o] = backward(o, g_recv[o, :, :queries]).astype(link_dtype)
-        qg_copy(o).start()
+        backward(o, g_recv[o, :, :queries])
 
     v_p = pv[...]
     g_p = pgrad[...]
     raw_g = (g_p - v_p * jnp.sum(v_p * g_p, axis=1, keepdims=True)) / plen[...]
     term = lax.dot_general(
-        raw_g.astype(jnp.bfloat16), ph_ref[...].reshape(p_rows, width), TN,
+        raw_g.astype(jnp.bfloat16), ph_ref[...], TN,
         preferred_element_type=jnp.float32,
     )
 
@@ -298,7 +288,7 @@
         ),
     )(
         query_hidden,
-        jnp.transpose(passage_hidden, (1, 0, 2)),
+        jnp.transpose(passage_hidden, (1, 0, 2)).reshape(p_rows, width),
         projection,
         teacher_rows,
         teacher_pos.reshape(1, queries),

time: 50.2 us -> 48.4 us (0.964)
  Pallas kernels: 41.8 us -> 40 us
    pallas_call x1, Pallas kernels: 41.8 us -> 40 us  [per_device(): pl.pallas_call(functools.partial(kernel, n, link_dtype), out_shape=(jax.S...]
where the time goes in v3:
time: 48.4 us; the launch traced here: 48.1 us
  Pallas kernels  40 us (83%)
  local copies, waits for them, and re-layouts  7.46 us (15%)
  between operations  0.66 us (1%)
    pallas_call x1, Pallas kernels, per_device(): pl.pallas_call(functools.partial(kernel, n, link_dtype), out_shape=(jax.S...  40 us
    unnamed x16, local copies, waits for them, and re-layouts  7.46 us

profile of v3, /device:TPU:0, one launch (start us, length us, event | category | flops | bytes accessed | tf_op | source)
XLA Modules:
  0.0 48.1 jit_solution(11169026704602966618)
XLA Ops:
  0.6 0.0 copy-start
  0.6 1.6 %copy-done = bf16[8,180,768]{2,0,1:T(8,128)(2,1)S(1)} copy-done((bf16[8,180,768]{2,0,1:T(8,128)(2,1)S(1)}, bf16[8,180,768]{2,0,1:T(8,128)(2,1)}, u32[]{:S(2)}) %copy-start) | copy-done | bytes 2211864
  2.3 0.0 copy-start.1
  2.3 1.1 %copy-done.1 = bf16[16,32,768]{2,1,0:T(8,128)(2,1)S(1)} copy-done((bf16[16,32,768]{2,1,0:T(8,128)(2,1)S(1)}, bf16[16,32,768]{2,1,0:T(8,128)(2,1)}, u32[]{:S(2)}) %copy-start.1) | copy-done | bytes 786456
  3.4 0.0 copy-start.2
  3.4 0.9 %copy-done.2 = bf16[768,128]{1,0:T(8,128)(2,1)S(1)} copy-done((bf16[768,128]{1,0:T(8,128)(2,1)S(1)}, bf16[768,128]{1,0:T(8,128)(2,1)}, u32[]{:S(2)}) %copy-start.2) | copy-done | bytes 196632
  4.3 0.0 copy-start.3
  4.3 0.7 %copy-done.3 = f32[16,32]{1,0:T(8,128)S(1)} copy-done((f32[16,32]{1,0:T(8,128)S(1)}, f32[16,32]{1,0:T(8,128)}, u32[]{:S(2)}) %copy-start.3) | copy-done | bytes 2072
  5.0 0.0 copy-start.4
  5.0 0.7 %copy-done.4 = s32[16]{0:T(128)S(1)} copy-done((s32[16]{0:T(128)S(1)}, s32[16]{0:T(128)}, u32[]{:S(2)}) %copy-start.4) | copy-done | bytes 88
  5.7 0.0 copy-start.5
  5.7 0.7 %copy-done.5 = s32[16]{0:T(128)S(1)} copy-done((s32[16]{0:T(128)S(1)}, s32[16]{0:T(128)}, u32[]{:S(2)}) %copy-start.5) | copy-done | bytes 88
  6.3 0.0 copy-start.6
  6.3 0.7 %copy-done.6 = s32[8]{0:T(128)S(1)} copy-done((s32[8]{0:T(128)S(1)}, s32[8]{0:T(128)}, u32[]{:S(2)}) %copy-start.6) | copy-done | bytes 56
  7.0 40.0 %shard_map.86 = (f32[1,16]{1,0:T(1,128)S(1)}, f32[48,128]{1,0:T(8,128)S(1)}) custom-call(bf16[16,32,768]{2,1,0:T(8,128)(2,1)S(1)} %copy-done.1, bf16[1440,768]{1,0:T(8,128)(2,1)S(1)} %bitcast.7, bf16[768,128]{1,0:T(8,128)(2,1)S(1)} %copy-done.2, f32[16,32]{1,0:T(8,128)S(1)} %copy-done.3, s32[1,16]{1,0:T(1,128)S(1)} %bitcast.8, s32[1,16]{1,0:T(1,128)S(1)} %bitcast.9, ...), custom_call_target="tpu_custom_call" | custom-call | tf_op jit(solution)/shard_map/pallas_call | solution.py:249
  47.0 0.5 %copy.11 = f32[16]{0:T(128)} copy(f32[16]{0:T(128)S(1)} %bitcast.11) | data formatting | bytes 128
  47.5 0.6 %copy.12 = f32[48,128]{1,0:T(8,128)} copy(f32[48,128]{1,0:T(8,128)S(1)} %get-tuple-element.9) | data formatting | bytes 49152
Async XLA Ops:
  0.6 1.6 %copy-start = (bf16[8,180,768]{2,0,1:T(8,128)(2,1)S(1)}, bf16[8,180,768]{2,0,1:T(8,128)(2,1)}, u32[]{:S(2)}) copy-start(bf16[8,180,768]{2,0,1:T(8,128)(2,1)} %param.8) | copy-start | bytes 6635524
  2.3 1.1 %copy-start.1 = (bf16[16,32,768]{2,1,0:T(8,128)(2,1)S(1)}, bf16[16,32,768]{2,1,0:T(8,128)(2,1)}, u32[]{:S(2)}) copy-start(bf16[16,32,768]{2,1,0:T(8,128)(2,1)} %qh_ref.1) | copy-start | bytes 2359300
  3.4 0.9 %copy-start.2 = (bf16[768,128]{1,0:T(8,128)(2,1)S(1)}, bf16[768,128]{1,0:T(8,128)(2,1)}, u32[]{:S(2)}) copy-start(bf16[768,128]{1,0:T(8,128)(2,1)} %proj_ref.1) | copy-start | bytes 589828
  4.3 0.7 %copy-start.3 = (f32[16,32]{1,0:T(8,128)S(1)}, f32[16,32]{1,0:T(8,128)}, u32[]{:S(2)}) copy-start(f32[16,32]{1,0:T(8,128)} %rows_ref.1) | copy-start | bytes 6148
  5.0 0.7 %copy-start.4 = (s32[16]{0:T(128)S(1)}, s32[16]{0:T(128)}, u32[]{:S(2)}) copy-start(s32[16]{0:T(128)} %param.11) | copy-start | bytes 196
  5.7 0.7 %copy-start.5 = (s32[16]{0:T(128)S(1)}, s32[16]{0:T(128)}, u32[]{:S(2)}) copy-start(s32[16]{0:T(128)} %param.12) | copy-start | bytes 196
  6.3 0.7 %copy-start.6 = (s32[8]{0:T(128)S(1)}, s32[8]{0:T(128)}, u32[]{:S(2)}) copy-start(s32[8]{0:T(128)} %param.13) | copy-start | bytes 100

commit v4 on v1

--- a/solution.py
+++ b/solution.py
@@ -1,5 +1,4 @@
 import functools
-import math
 
 import jax
 import jax.numpy as jnp
@@ -11,7 +10,6 @@
 CYCLE = 4
 HEAT = 0.05
 EPSILON = 1e-06
-EXP2_SCALE = math.log2(math.e) / HEAT
 NT = (((1,), (1,)), ((), ()))
 TN = (((0,), (0,)), ((), ()))
 
@@ -113,11 +111,11 @@
     def score(o):
         units = q_all[o]
 
-        @pl.loop(0, passages)
+        @pl.loop(0, passages, unroll=8)
         def _(p):
             at = pl.ds(pl.multiple_of(p * padded, padded), padded)
             sims = lax.dot_general(pu[at], units, NT, preferred_element_type=jnp.float32)
-            e = jnp.where(token < len_ref[0, p], jnp.exp2(sims * EXP2_SCALE), 0.0)
+            e = jnp.where(token < len_ref[0, p], jnp.exp(sims * (1.0 / HEAT)), 0.0)
             exps[o, at] = e
             den[o, pl.ds(p, 1)] = jnp.sum(e, axis=0, keepdims=True)
 
@@ -163,7 +161,7 @@
         units = q_all[o]
         den[o] = dot32(grads, spread, (((1,), (0,)), ((), ()))) / den[o]
 
-        @pl.loop(0, passages)
+        @pl.loop(0, passages, unroll=8)
         def _(p):
             at = pl.ds(pl.multiple_of(p * padded, padded), padded)
             w = (exps[o, at] * den[o, pl.ds(p, 1)]).astype(jnp.bfloat16)

time: 45.4 us -> 43 us (0.947)
  Pallas kernels: 41.2 us -> 38.8 us
    pallas_call x1, Pallas kernels: 41.2 us -> 38.8 us  [per_device(): pl.pallas_call(functools.partial(kernel, n, link_dtype), out_shape=(jax.S...]
where the time goes in v4:
time: 43 us; the launch traced here: 42.8 us
  Pallas kernels  38.8 us (90%)
  local copies, waits for them, and re-layouts  3.28 us (8%)
  between operations  0.74 us (2%)
    pallas_call x1, Pallas kernels, per_device(): pl.pallas_call(functools.partial(kernel, n, link_dtype), out_shape=(jax.S...  38.8 us
    unnamed x15, local copies, waits for them, and re-layouts  3.28 us

profile of v4, /device:TPU:0, one launch (start us, length us, event | category | flops | bytes accessed | tf_op | source)
XLA Modules:
  0.0 42.8 jit_solution(12109080351968153122)
XLA Ops:
  0.6 0.0 copy-start.5
  0.6 0.0 copy-start.4
  0.7 0.0 copy-start.3
  0.7 0.0 copy-start.2
  0.7 0.0 copy-start.1
  0.7 0.0 copy-start
  0.7 2.1 %copy.9.ph_ref = bf16[8,180,768]{2,1,0:T(8,128)(2,1)S(1)} copy(bf16[8,180,768]{2,0,1:T(8,128)(2,1)} %param.8) | data formatting | bytes 4423680 | tf_op args[1]
  2.8 0.0 copy-done.5
  2.8 0.0 copy-done.4
  2.8 0.0 copy-done.3
  2.9 0.0 copy-done.2
  2.9 0.0 copy-done.1
  2.9 0.0 copy-done
  2.9 38.8 %shard_map.86 = (f32[1,16]{1,0:T(1,128)S(1)}, f32[48,128]{1,0:T(8,128)S(1)}) custom-call(bf16[16,32,768]{2,1,0:T(8,128)(2,1)S(1)} %copy-done, bf16[8,180,768]{2,1,0:T(8,128)(2,1)S(1)} %copy.9.ph_ref, bf16[768,128]{1,0:T(8,128)(2,1)S(1)} %copy-done.1, f32[16,32]{1,0:T(8,128)S(1)} %copy-done.2, s32[1,16]{1,0:T(1,128)S(1)} %bitcast.4, s32[1,16]{1,0:T(1,128)S(1)} %bitcast.5, ...), custom_call_target="tpu_custom_call" | custom-call | tf_op jit(solution)/shard_map/pallas_call | solution.py:249
  41.7 0.5 %copy.12 = f32[16]{0:T(128)} copy(f32[16]{0:T(128)S(1)} %bitcast.7) | data formatting | bytes 128
  42.2 0.6 %copy.13 = f32[48,128]{1,0:T(8,128)} copy(f32[48,128]{1,0:T(8,128)S(1)} %get-tuple-element.9) | data formatting | bytes 49152
Async XLA Ops:
  0.6 2.2 %copy-start.5 = (s32[8]{0:T(128)S(1)}, s32[8]{0:T(128)}, u32[]{:S(2)}) copy-start(s32[8]{0:T(128)} %param.13) | copy-start | bytes 100
  0.6 2.2 %copy-start.4 = (s32[16]{0:T(128)S(1)}, s32[16]{0:T(128)}, u32[]{:S(2)}) copy-start(s32[16]{0:T(128)} %param.12) | copy-start | bytes 196
  0.7 2.2 %copy-start.3 = (s32[16]{0:T(128)S(1)}, s32[16]{0:T(128)}, u32[]{:S(2)}) copy-start(s32[16]{0:T(128)} %param.11) | copy-start | bytes 196
  0.7 2.2 %copy-start.2 = (f32[16,32]{1,0:T(8,128)S(1)}, f32[16,32]{1,0:T(8,128)}, u32[]{:S(2)}) copy-start(f32[16,32]{1,0:T(8,128)} %rows_ref.1) | copy-start | bytes 6148
  0.7 2.2 %copy-start.1 = (bf16[768,128]{1,0:T(8,128)(2,1)S(1)}, bf16[768,128]{1,0:T(8,128)(2,1)}, u32[]{:S(2)}) copy-start(bf16[768,128]{1,0:T(8,128)(2,1)} %proj_ref.1) | copy-start | bytes 589828
  0.7 2.2 %copy-start = (bf16[16,32,768]{2,1,0:T(8,128)(2,1)S(1)}, bf16[16,32,768]{2,1,0:T(8,128)(2,1)}, u32[]{:S(2)}) copy-start(bf16[16,32,768]{2,1,0:T(8,128)(2,1)} %qh_ref.1) | copy-start | bytes 2359300

commit v5 on v4

--- a/solution.py
+++ b/solution.py
@@ -24,7 +24,7 @@
     n, link_dtype,
     qh_ref, ph_ref, proj_ref, rows_ref, pos_ref, cnt_ref, len_ref,
     loss_ref, grad_ref,
-    teach_own, teach_all, qraw, q_all, pv, plen, pu, exps, den, w_buf, pgrad,
+    teach_own, teach_all, qraw, q_all, pv, plen, pu, put, exps, den, w_buf, pgrad,
     s_send, s_recv, g_send, g_recv, qg_send, qg_recv, part, part_own, part_recv,
     teach_ss, teach_rs, q_ss, q_rs, s_ss, s_rs, g_ss, g_rs, qg_ss, qg_rs, part_ss, part_rs,
 ):
@@ -66,7 +66,7 @@
     def q_copy(o):
         return remote(q_all.at[0], q_all.at[o], q_ss.at[o], q_rs.at[o], peer(o))
 
-    for o in range(1, CYCLE):
+    for o in reversed(range(1, CYCLE)):
         q_copy(o).start()
 
     def teach_send(k):
@@ -89,6 +89,7 @@
         pv[at : at + p_tokens] = raw_p / length
         plen[at : at + p_tokens] = jnp.broadcast_to(length, raw_p.shape)
     pu[...] = pv[...].astype(jnp.bfloat16)
+    put[...] = jnp.transpose(pv[...]).astype(jnp.bfloat16)
     pgrad[...] = jnp.zeros(pgrad.shape, jnp.float32)
 
     low = lax.broadcasted_iota(jnp.int32, (queries, q_rows), 0) * q_tokens
@@ -166,15 +167,18 @@
             at = pl.ds(pl.multiple_of(p * padded, padded), padded)
             w = (exps[o, at] * den[o, pl.ds(p, 1)]).astype(jnp.bfloat16)
             w_buf[at] = w
-            pgrad[at] += jnp.dot(w, units, preferred_element_type=jnp.float32)
-
-        return lax.dot_general(pu[...], w_buf[...], TN, preferred_element_type=jnp.float32)
+
+        q_grad = jnp.dot(put[...], w_buf[...], preferred_element_type=jnp.float32)
+        if o > 0:
+            qg_send[o] = q_grad.astype(link_dtype)
+            qg_copy(o).start()
+        pgrad[...] += jnp.dot(w_buf[...], units, preferred_element_type=jnp.float32)
+        return q_grad
 
     q_total = backward(0, score_grad[:passages])
-    for o in range(1, CYCLE):
+    for o in reversed(range(1, CYCLE)):
         g_copy(o).wait_recv()
-        qg_send[o] = backward(o, g_recv[o, :, :queries]).astype(link_dtype)
-        qg_copy(o).start()
+        backward(o, g_recv[o, :, :queries])
 
     term = jnp.zeros((dim, width), jnp.float32)
     for p in range(passages):
@@ -262,6 +266,7 @@
             pltpu.VMEM((p_rows, dim), f32),
             pltpu.VMEM((p_rows, dim), f32),
             pltpu.VMEM((p_rows, dim), bf16),
+            pltpu.VMEM((dim, p_rows), bf16),
             pltpu.VMEM((CYCLE, p_rows, q_rows), f32),
             pltpu.VMEM((CYCLE, passages, q_rows), f32),
             pltpu.VMEM((p_rows, q_rows), bf16),

time: 43 us -> 47.6 us (1.11)
  Pallas kernels: 38.8 us -> 43.4 us
    pallas_call x1, Pallas kernels: 38.8 us -> 43.4 us  [per_device(): pl.pallas_call(functools.partial(kernel, n, link_dtype), out_shape=(jax.S...]
where the time goes in v5:
time: 47.6 us; the launch traced here: 47.4 us
  Pallas kernels  43.4 us (91%)
  local copies, waits for them, and re-layouts  3.28 us (7%)
  between operations  0.74 us (2%)
    pallas_call x1, Pallas kernels, per_device(): pl.pallas_call(functools.partial(kernel, n, link_dtype), out_shape=(jax.S...  43.4 us
    unnamed x15, local copies, waits for them, and re-layouts  3.28 us

profile of v5, /device:TPU:0, one launch (start us, length us, event | category | flops | bytes accessed | tf_op | source)
XLA Modules:
  0.0 47.4 jit_solution(5605058202666805648)
XLA Ops:
  0.6 0.0 copy-start.5
  0.6 0.0 copy-start.4
  0.7 0.0 copy-start.3
  0.7 0.0 copy-start.2
  0.7 0.0 copy-start.1
  0.7 0.0 copy-start
  0.7 2.1 %copy.9.ph_ref = bf16[8,180,768]{2,1,0:T(8,128)(2,1)S(1)} copy(bf16[8,180,768]{2,0,1:T(8,128)(2,1)} %param.8) | data formatting | bytes 4423680 | tf_op args[1]
  2.8 0.0 copy-done.5
  2.8 0.0 copy-done.4
  2.8 0.0 copy-done.3
  2.9 0.0 copy-done.2
  2.9 0.0 copy-done.1
  2.9 0.0 copy-done
  2.9 43.4 %shard_map.86 = (f32[1,16]{1,0:T(1,128)S(1)}, f32[48,128]{1,0:T(8,128)S(1)}) custom-call(bf16[16,32,768]{2,1,0:T(8,128)(2,1)S(1)} %copy-done, bf16[8,180,768]{2,1,0:T(8,128)(2,1)S(1)} %copy.9.ph_ref, bf16[768,128]{1,0:T(8,128)(2,1)S(1)} %copy-done.1, f32[16,32]{1,0:T(8,128)S(1)} %copy-done.2, s32[1,16]{1,0:T(1,128)S(1)} %bitcast.4, s32[1,16]{1,0:T(1,128)S(1)} %bitcast.5, ...), custom_call_target="tpu_custom_call" | custom-call | tf_op jit(solution)/shard_map/pallas_call | solution.py:253
  46.3 0.5 %copy.12 = f32[16]{0:T(128)} copy(f32[16]{0:T(128)S(1)} %bitcast.7) | data formatting | bytes 128
  46.8 0.6 %copy.13 = f32[48,128]{1,0:T(8,128)} copy(f32[48,128]{1,0:T(8,128)S(1)} %get-tuple-element.9) | data formatting | bytes 49152
Async XLA Ops:
  0.6 2.2 %copy-start.5 = (s32[8]{0:T(128)S(1)}, s32[8]{0:T(128)}, u32[]{:S(2)}) copy-start(s32[8]{0:T(128)} %param.13) | copy-start | bytes 100
  0.6 2.2 %copy-start.4 = (s32[16]{0:T(128)S(1)}, s32[16]{0:T(128)}, u32[]{:S(2)}) copy-start(s32[16]{0:T(128)} %param.12) | copy-start | bytes 196
  0.7 2.2 %copy-start.3 = (s32[16]{0:T(128)S(1)}, s32[16]{0:T(128)}, u32[]{:S(2)}) copy-start(s32[16]{0:T(128)} %param.11) | copy-start | bytes 196
  0.7 2.2 %copy-start.2 = (f32[16,32]{1,0:T(8,128)S(1)}, f32[16,32]{1,0:T(8,128)}, u32[]{:S(2)}) copy-start(f32[16,32]{1,0:T(8,128)} %rows_ref.1) | copy-start | bytes 6148
  0.7 2.2 %copy-start.1 = (bf16[768,128]{1,0:T(8,128)(2,1)S(1)}, bf16[768,128]{1,0:T(8,128)(2,1)}, u32[]{:S(2)}) copy-start(bf16[768,128]{1,0:T(8,128)(2,1)} %proj_ref.1) | copy-start | bytes 589828
  0.7 2.2 %copy-start = (bf16[16,32,768]{2,1,0:T(8,128)(2,1)S(1)}, bf16[16,32,768]{2,1,0:T(8,128)(2,1)}, u32[]{:S(2)}) copy-start(bf16[16,32,768]{2,1,0:T(8,128)(2,1)} %qh_ref.1) | copy-start | bytes 2359300
